TPU v7x, 256 devices: a whole 4x4x8 slice. The times are simulated.
256 devices in a mesh: pitch: 16 (over x_lo, z), radial: 8 (over y, core), axial: 2 (over x_hi).
Axes of the slice: x: 4 (x_hi: 2, x_lo: 2; x = x_hi * 2 + x_lo), y: 4, z: 8, core: 2. Of those that a mesh axis runs over, the one named last changes fastest.
Arguments:
- density: float32 [9, 4, 64, 2048], P(None, 'axial', 'radial', 'pitch'), may hold values from 0.5 to 2
- moments: float32 [9, 4, 4, 64, 2048], P(None, None, 'axial', 'radial', 'pitch'), may hold values from -6 to 6
- shifts: int32 [9], replicated, may hold values from 0 to 2047, as said below
Outputs:
- residual: float32 [9, 5, 4, 64, 2048], P(None, None, 'axial', 'radial', 'pitch')
- update: float32 [9, 5, 4, 64, 2048], P(None, None, 'axial', 'radial', 'pitch')
Inputs may be any that keep to these rules, and one draw needn't show every extreme that they name: `shifts`: every instance's offset lies in 0 to 2047 and some instance has offset 2048 - 1.
All inputs are finite; a program needn't handle non-finite values.
Results may differ from a plain program's by a relative error of at most 0.0005.
Values sent between devices are 32-bit elements; how exact they have to be, the bound alone decides.
No kernel may reach another device: no remote copies, remote signals or barrier semaphores. Data moves between devices by JAX's collectives and lax.ppermute only.
A program may use at most 192 MiB of HBM per device.

v0:
```python
import math
import jax
import jax.numpy as jnp
import numpy as np
from jax import lax
from jax.sharding import PartitionSpec as P

COEFFS = (0.75, -0.15, 1.0 / 60.0)
GAMMA_LESS = 0.4
HIGHEST = lax.Precision.HIGHEST


def padded_2(x, sides, width, wrap):
    for axis, dim in sides:
        devices, length = (lax.axis_size(axis), x.shape[dim])
        up = [(i, (i + 1) % devices) for i in range(devices if wrap else devices - 1)]
        down = [(j, i) for i, j in up]
        last = lax.slice_in_dim(x, length - width, length, axis=dim)
        leading = lax.slice_in_dim(x, 0, width, axis=dim)
        before = lax.ppermute(last, axis, up)
        after = lax.ppermute(leading, axis, down)
        x = jnp.concatenate([before, x, after], axis=dim)
    return x


def carried_in(x, axis, combine, identity, reverse):
    devices, position = (lax.axis_size(axis), lax.axis_index(axis))
    everything = jax.tree.map(lambda part: lax.all_gather(part, axis), x)
    start = jax.tree.map(
        lambda part, zero: jnp.broadcast_to(jnp.asarray(zero, part.dtype), part.shape), x, identity
    )

    def hop(k, before):
        at = devices - 1 - k if reverse else k
        reached = at > position if reverse else at < position
        new = combine(before, jax.tree.map(lambda part: part[at], everything))
        return jax.tree.map(lambda a, b: jnp.where(reached, a, b), new, before)

    return lax.fori_loop(0, devices, hop, start)


def from_partner(x, axis, apart):
    return lax.ppermute(x, axis, [(i, i ^ 1 << apart) for i in range(lax.axis_size(axis))])


def spectral_table(count):
    points = np.arange(count)
    spread = points[:, None] - points[None, :]
    nonzero = np.where(spread == 0, 1, spread)
    entries = 0.5 * np.where(spread % 2 == 0, 1.0, -1.0) / np.sin(np.pi * nonzero / count)
    return jnp.asarray(np.where(spread == 0, 0.0, entries), jnp.float32)


def fluxes(density, moments):
    axial_m = moments[:, 0]
    radial_m = moments[:, 1]
    pitch_m = moments[:, 2]
    energy = moments[:, 3]
    pressure = GAMMA_LESS * (
        energy - 0.5 * (axial_m * axial_m + radial_m * radial_m + pitch_m * pitch_m) / density
    )
    pitch_v = pitch_m / density
    radial_v = radial_m / density
    along_pitch = jnp.stack(
        [
            pitch_m,
            axial_m * pitch_v,
            radial_m * pitch_v,
            pitch_m * pitch_v + pressure,
            (energy + pressure) * pitch_v,
        ],
        axis=1,
    )
    along_radial = jnp.stack(
        [
            radial_m,
            axial_m * radial_v,
            radial_m * radial_v + pressure,
            pitch_m * radial_v,
            (energy + pressure) * radial_v,
        ],
        axis=1,
    )
    return (along_pitch, along_radial)


def stencil(padded, axis, length):
    summed = None
    for offset, weight in enumerate(COEFFS):
        reach = offset + 1
        ahead = lax.slice_in_dim(padded, 3 + reach, 3 + reach + length, axis=axis)
        behind = lax.slice_in_dim(padded, 3 - reach, 3 - reach + length, axis=axis)
        term = weight * (ahead - behind)
        summed = term if summed is None else summed + term
    return summed


def pitch_derivative(along_pitch):
    width = along_pitch.shape[-1]
    edges = jnp.concatenate([along_pitch[..., :3], along_pitch[..., width - 3 :]], axis=4)
    rims = padded_2(edges, (("pitch", 4),), 3, True)
    inner = None
    for offset, weight in enumerate(COEFFS):
        reach = offset + 1
        term = weight * (
            jnp.roll(along_pitch, -reach, axis=4) - jnp.roll(along_pitch, reach, axis=4)
        )
        inner = term if inner is None else inner + term
    left_strip = jnp.concatenate([rims[..., 0:3], along_pitch[..., :6]], axis=4)
    right_strip = jnp.concatenate([along_pitch[..., width - 6 :], rims[..., 9:12]], axis=4)
    left_cols = stencil(left_strip, 4, 3)
    right_cols = stencil(right_strip, 4, 3)
    pad_none = ((0, 0),) * 4
    left_full = jnp.pad(left_cols, pad_none + ((0, width - 3),))
    right_full = jnp.pad(right_cols, pad_none + ((width - 3, 0),))
    column = jnp.arange(width)
    return jnp.where(column < 3, left_full, jnp.where(column >= width - 3, right_full, inner))


def cut_rows(joined, starts, width):
    pieces = []
    for member in range(joined.shape[0]):
        opening = starts[member]
        pieces.append(lax.dynamic_slice_in_dim(joined[member], opening, width, axis=2))
    return jnp.stack(pieces, axis=0)


def carry_in(sums, backward, width, decay):
    count_p = lax.axis_size("pitch")
    place = lax.axis_index("pitch")
    step_log = width * math.log(decay)
    wrap_gain = 1.0 / (1.0 - decay ** (width * count_p))
    position = count_p - 1 - place if backward else place
    factor = jnp.full((1,), decay**width, jnp.float32)

    def combine(earlier, later):
        return (earlier[0] * later[0], later[1] + later[0] * earlier[1])

    scanned = carried_in(
        (factor, sums),
        "pitch",
        combine,
        (jnp.ones((1,), jnp.float32), jnp.zeros_like(sums)),
        backward,
    )
    weighted = sums * jnp.exp((count_p - 1 - position).astype(jnp.float32) * step_log)
    circuit = lax.psum(weighted, "pitch")
    return scanned[1] + jnp.exp(position.astype(jnp.float32) * step_log) * wrap_gain * circuit


def smooth(residual):
    width = residual.shape[-1]
    extent = width * lax.axis_size("pitch")
    smooth_eps = float(extent * extent // 16)
    decay = 2.0 * smooth_eps / (1.0 + 2.0 * smooth_eps + math.sqrt(1.0 + 4.0 * smooth_eps))
    points = np.arange(width)
    spacing = points[None, :] - points[:, None]
    lower = np.where(spacing >= 0, decay ** np.maximum(spacing, 0), 0.0)
    forward_table = jnp.asarray(lower, jnp.float32)
    backward_table = jnp.asarray(lower.T, jnp.float32)
    rising = jnp.asarray(decay ** (points + 1.0), jnp.float32)
    falling = jnp.asarray(decay ** (width - points + 0.0), jnp.float32)
    flat = residual.reshape(-1, width)
    first_pass = jnp.dot(flat, forward_table, precision=HIGHEST, preferred_element_type=jnp.float32)
    carried = carry_in(first_pass[:, -1], False, width, decay)
    swept = first_pass + carried[:, None] * rising[None, :]
    second_pass = jnp.dot(
        swept, backward_table, precision=HIGHEST, preferred_element_type=jnp.float32
    )
    carried_back = carry_in(second_pass[:, 0], True, width, decay)
    result = (second_pass + carried_back[:, None] * falling[None, :]) * (decay / smooth_eps)
    return result.reshape(residual.shape)


def local(density, moments, shifts):
    fields = jnp.concatenate([density[:, None], moments], axis=1)
    along_pitch, along_radial = fluxes(density, moments)
    count_p = lax.axis_size("pitch")
    place = lax.axis_index("pitch")
    width = density.shape[-1]
    planes = density.shape[1]
    padded_r = padded_2(along_radial, (("radial", 3),), 3, False)
    residual = pitch_derivative(along_pitch) + stencil(padded_r, 3, density.shape[2])
    residual = residual + jnp.einsum(
        "nm,mvarp->nvarp", spectral_table(fields.shape[0]), fields, precision=HIGHEST
    )
    stator = lax.axis_index("axial") == 1
    edge = jnp.where(stator, fields[:, :, 0], fields[:, :, planes - 1])
    facing = from_partner(edge, "axial", 0)
    extent = width * count_p
    offsets = jnp.where(stator, shifts, (extent - shifts) % extent)
    whole = lax.all_gather(facing, "pitch", axis=3, tiled=True)
    joined = jnp.concatenate([whole, whole], axis=3)
    aligned = cut_rows(joined, (place * width - offsets) % extent, width)
    penalty = aligned - edge
    target = jnp.where(stator, 0, planes - 1)
    chosen = (jnp.arange(planes) == target).astype(jnp.float32)
    residual = residual + penalty[:, :, None] * chosen[None, None, :, None, None]
    update = smooth(residual)
    return (residual, update)


def solution(mesh):
    in_specs = (P(None, "axial", "radial", "pitch"), P(None, None, "axial", "radial", "pitch"), P())
    out_specs = (
        P(None, None, "axial", "radial", "pitch"),
        P(None, None, "axial", "radial", "pitch"),
    )
    return jax.shard_map(local, mesh=mesh, in_specs=in_specs, out_specs=out_specs, check_vma=False)
```

profile of v0, /device:TPU:8, one launch (start us, length us, event | category | flops | bytes accessed | tf_op | source)
XLA Modules:
  0.0 391.4 jit_solution(6950493124615744178)
XLA Ops:
  7.2 1.1 copy.155
  8.4 1.0 copy.166
  9.4 3.1 collective-permute-start.4
  12.5 1.7 fusion.59
  14.2 1.3 copy.143
  15.9 1.1 constant_dynamic-update-slice_fusion
  17.0 1.3 copy.162
  18.3 1.3 copy.163
  19.6 1.1 constant_dynamic-update-slice_fusion.1
  20.6 2.4 fusion.24
  23.0 2.2 copy.146
  25.2 2.4 bitcast_dynamic-update-slice_fusion.7
  27.6 2.8 bitcast_dynamic-update-slice_fusion.6
  30.4 0.7 multiply_divide_fusion
  31.1 2.2 copy.148
  33.3 1.4 copy.164
  34.7 2.9 bitcast_dynamic-update-slice_fusion.5
  38.2 3.0 bitcast_dynamic-update-slice_fusion.4
  41.2 1.7 fusion.52
  42.9 1.9 collective-permute-start
  44.8 4.0 %collective-permute-start.1 = (f32[9,5,2,8,3]{0,3,4,2,1:T(8,128)}, f32[9,5,2,8,3]{0,3,4,2,1:T(8,128)}, u32[]{:S(2)}, u32[]{:S(2)}) collective-permute-start(f32[9,5,2,8,3]{0,3,4,2,1:T(8,128)} %get-tuple-element.323), channel_id=1, source_target_pairs={{16,0},{32,16},{48,32},{64,48},{80,64},{96,80},{112,96},{128,112},... | collective-permute-start | bytes 25928 | tf_op jit(solution)/shard_map/ppermute | solution.py:21
  49.3 2.3 copy-done.1
  51.6 2.6 fusion.58
  54.1 3.5 copy.150
  57.6 1.9 collective-permute-start.2
  59.6 2.2 copy.152
  61.8 2.4 collective-permute-start.3
  64.8 0.7 fusion.60
  65.5 1.4 fusion.56
  66.9 1.6 fusion.54
  68.5 1.6 fusion.27
  70.1 1.3 fusion.51
  71.4 8.8 %fusion.53 = (f32[9,5,2,8,125]{0,3,4,2,1:T(8,128)}, f32[9,5,2,8,125]{0,3,4,2,1:T(8,128)}) fusion(f32[9,5,2,8,128]{0,3,4,2,1:T(8,128)} %get-tuple-element.336), kind=kLoop, calls=%fused_computation.138 | loop fusion | bytes 1440000 | tf_op jit(solution)/shard_map/jit(_roll_static)/slice | solution.py:106
  80.2 4.7 %fusion.55 = (f32[9,5,2,8,126]{0,3,4,2,1:T(8,128)}, f32[9,5,2,8,126]{0,3,4,2,1:T(8,128)}) fusion(f32[9,5,2,8,128]{0,3,4,2,1:T(8,128)S(1)} %bitcast.139), kind=kLoop, calls=%fused_computation.140 | loop fusion | bytes 1451520 | tf_op jit(solution)/shard_map/jit(_roll_static)/slice | solution.py:106
  84.9 4.6 %fusion.57 = (f32[9,5,2,8,127]{0,3,4,2,1:T(8,128)}, f32[9,5,2,8,127]{0,3,4,2,1:T(8,128)}) fusion(f32[9,5,2,8,128]{0,3,4,2,1:T(8,128)S(1)} %bitcast.139), kind=kLoop, calls=%fused_computation.142 | loop fusion | bytes 1463040 | tf_op jit(solution)/shard_map/jit(_roll_static)/slice | solution.py:106
  101.0 3.2 copy.156
  111.0 0.8 dynamic-update-slice.1
  111.9 2.1 fusion.42
  114.0 2.7 copy.151
  116.7 3.3 copy.153
  120.0 14.6 %all-gather.4.cloned.1.call-done = f32[9,5,8,2048]{3,0,2,1:T(8,128)} async-done(((f32[9,5,8,128]{3,0,2,1:T(8,128)}), f32[9,5,8,2048]{3,0,2,1:T(8,128)}) %all-gather.4.cloned.1.call-update) | async-done | bytes 2949136 | tf_op jit(solution)/shard_map/all_gather | solution.py:192
  134.6 5.7 %constant_dynamic-update-slice_fusion.3 = f32[9,5,8,4096]{3,0,2,1:T(8,128)} fusion(f32[9,5,8,2048]{3,0,2,1:T(8,128)} %all-gather.4.cloned.1.call-done), kind=kLoop, calls=%fused_computation.110 | loop fusion | bytes 8192000
  140.3 3.0 constant_dynamic-update-slice_fusion.2
  143.3 20.9 %fusion.50 = (f32[1,5,8,4096]{3,0,2,1:T(1,128)}, f32[1,5,8,4096]{3,0,2,1:T(1,128)}, f32[1,5,8,4096]{3,0,2,1:T(1,128)}, f32[1,5,8,4096]{3,0,2,1:T(1,128)}, f32[1,...) fusion(f32[9,5,8,4096]{3,0,2,1:T(8,128)} %constant_dynamic-upda, ...), kind=kLoop, calls=%fused_computation.135 | loop fusion | bytes 11796480 | tf_op jit(solution)/shard_map/slice | solution.py:124
  164.2 0.9 dynamic-slice_bitcast_fusion.8
  165.1 1.6 dynamic-slice_bitcast_fusion
  166.7 1.6 dynamic-slice_bitcast_fusion.2
  168.3 1.6 dynamic-slice_bitcast_fusion.4
  169.9 1.6 dynamic-slice_bitcast_fusion.6
  171.4 1.8 stack.79
  173.3 0.8 subtract_bitcast_fusion
  174.0 3.3 copy.157
  177.3 35.9 %fusion.7 = f32[9,5,2,8,128]{0,3,4,2,1:T(8,128)} fusion(f32[9,5,2,8,128]{0,3,4,2,1:T(8,128)} %copy.156, f32[9,5,2,8,128]{0,3,4,2,1:T(8,128)} %copy-done.1, f32[9,5,2,3,128]{0,3,4,2,1:T(4,128)} %copy.153, f32[9,5,2,3,128]{0,3,4,2,1:T(4,128)S(1)} %copy.151, f32[9,5,2,8,1]{0,3,4,2,1:T(8,128)} %get-tuple-element.331, ...), kind=kLoop, calls=%fused_computation.21 | loop fusion | flops 3133440 | bytes 3796104 | tf_op jit(solution)/shard_map/add | solution.py:198
  213.2 3.4 copy.159
  217.8 63.2 %all-reduce.6 = (f32[11520]{0:T(1024)S(1)}, f32[16]{0:T(128)S(1)}, f32[720]{0:T(1024)S(1)}) all-reduce(f32[11520]{0:T(1024)S(1)} %dynamic-update-slice, f32[16]{0:T(128)S(1)} %dynamic-update-slice.1, f32[720]{0:T(1024)S(1)} %get-tuple-element.282), channel_id=2, replica_groups=mesh['pitch'=16,'radial'=8,'axial'=2] {'pitch'}, use_global_device_ids=true, to_apply=%add.2 | all-reduce | flops 12256 | bytes 98048
  281.1 20.6 %while.30 = (s32[]{:T(128)}, f32[720]{0:T(1024)S(1)}, s32[]{:T(128)}, f32[16,720]{1,0:T(8,128)S(1)}, f32[16,1]{0,1:T(1,128)S(1)}, /*index=5*/s32[]{:T(128)}, s32[]{:T(128)}) while((s32[]{:T(128)}, f32[720]{0:T(1024)S(1)}, s32[]{:T(128)}, f32[16,720]{1,0:T(8,128)S(1)}, f32[16,1]{0,1:T(1,128)S(1)}, /*index=5*/s32[]{:T(128)}, ...), condition=%wide.region_1.2_spmd.clone, body=%wide.region_0.1_spmd.clone.sunk | while | flops 2884 | bytes 14517 | solution.py:39
  286.9 0.7 add_select_fusion.4
  288.1 0.7 add_select_fusion.4
  289.4 0.7 add_select_fusion.4
  298.4 0.7 add_select_fusion.4
  299.7 0.7 add_select_fusion.4
  302.8 59.9 %all-reduce.5 = (f32[11520]{0:T(1024)S(1)}, f32[720]{0:T(1024)S(1)}) all-reduce(f32[11520]{0:T(1024)S(1)} %dynamic-update-slice.2, f32[720]{0:T(1024)S(1)} %get-tuple-element.280), channel_id=3, replica_groups=mesh['pitch'=16,'radial'=8,'axial'=2] {'pitch'}, use_global_device_ids=true, to_apply=%add.4 | all-reduce | flops 12240 | bytes 97920
  362.9 20.7 %while.31 = (s32[]{:T(128)}, f32[720]{0:T(1024)S(1)}, s32[]{:T(128)}, f32[16,720]{1,0:T(8,128)S(1)}, f32[16,1]{0,1:T(1,128)S(1)}, /*index=5*/s32[]{:T(128)}, s32[]{:T(128)}, s32[]{:T(128)}, s32[]{:T(128)}) while((s32[]{:T(128)}, f32[720]{0:T(1024)S(1)}, s32[]{:T(128)}, f32[16,720]{1,0:T(8,128)S(1)}, f32[16,1]{0,1:T(1,128)S(1)}, ...), condition=%wide.region_4.5_spmd.clone, body=%wide.region_3.4_spmd.clone.sunk | while | flops 2888 | bytes 14579 | solution.py:39
  383.6 0.9 add_multiply_fusion
  (161 shorter events, 42.8 us)
Async XLA Ops:
  7.2 127.5 %all-gather.4.cloned.1.call-start = ((), (), s32[]{:S(2)}) async-start(), calls=%async_computation | async-start | bytes 5570560 | tf_op jit(solution)/shard_map/all_gather | solution.py:192
  8.4 4.2 %copy-start.5 = (f32[9,4,2,8,128]{4,0,3,2,1:T(8,128)}, f32[9,4,2,8,128]{4,0,3,2,1:T(8,128)S(1)}, u32[]{:S(2)}) copy-start(f32[9,4,2,8,128]{4,0,3,2,1:T(8,128)S(1)} %copy.155) | copy-start | bytes 884740
  9.4 3.2 copy-start.8
  9.4 25.2 %collective-permute-start.4 = (f32[9,5,8,128]{3,0,2,1:T(8,128)S(1)}, f32[9,5,8,128]{3,0,2,1:T(8,128)}, u32[]{:S(2)}, u32[]{:S(2)}) collective-permute-start(f32[9,5,8,128]{3,0,2,1:T(8,128)S(1)} %bitcast.141), channel_id=1, source_target_pairs={{0,1},{1,0},{2,3},{3,2},{4,5},{5,4},{6,7},{7,6},{8,9},{9,8},{10,11... | collective-permute-start | bytes 552968 | tf_op jit(solution)/shard_map/ppermute | solution.py:43
  25.2 5.2 %copy-start.9 = (f32[9,2,8,128]{3,2,1,0:T(8,128)S(1)}, f32[9,2,8,128]{3,2,1,0:T(8,128)}, u32[]{:S(2)}) copy-start(f32[9,2,8,128]{3,2,1,0:T(8,128)} %param.12) | copy-start | bytes 221188
  25.2 5.2 %copy-start.10 = (f32[9,2,8,128]{3,2,1,0:T(8,128)S(1)}, f32[9,2,8,128]{3,2,1,0:T(8,128)}, u32[]{:S(2)}) copy-start(f32[9,2,8,128]{3,2,1,0:T(8,128)} %copy.146) | copy-start | bytes 221188
  34.7 3.5 copy-start
  38.2 10.7 %copy-start.3 = (f32[9,2,8,128]{0,2,3,1:T(8,128)S(1)}, f32[9,2,8,128]{0,2,3,1:T(8,128)}, u32[]{:S(2)}) copy-start(f32[9,2,8,128]{0,2,3,1:T(8,128)} %copy.148) | copy-start | bytes 221188
  38.2 10.7 %copy-start.4 = (f32[9,1,2,8,128]{0,3,4,2,1:T(8,128)S(1)}, f32[9,1,2,8,128]{0,3,4,2,1:T(8,128)}, u32[]{:S(2)}) copy-start(f32[9,1,2,8,128]{0,3,4,2,1:T(8,128)} %copy.164) | copy-start | bytes 221188
  42.9 69.0 %collective-permute-start = (f32[9,5,2,8,3]{0,3,4,2,1:T(8,128)}, f32[9,5,2,8,3]{0,3,4,2,1:T(8,128)}, u32[]{:S(2)}, u32[]{:S(2)}) collective-permute-start(f32[9,5,2,8,3]{0,3,4,2,1:T(8,128)} %get-tuple-element.322), channel_id=1, source_target_pairs={{0,16},{16,32},{32,48},{48,64},{64,80},{80,96},{96,112},{112,128},... | collective-permute-start | bytes 25928 | tf_op jit(solution)/shard_map/ppermute | solution.py:20
  44.8 67.1 %collective-permute-start.1 = (f32[9,5,2,8,3]{0,3,4,2,1:T(8,128)}, f32[9,5,2,8,3]{0,3,4,2,1:T(8,128)}, u32[]{:S(2)}, u32[]{:S(2)}) collective-permute-start(f32[9,5,2,8,3]{0,3,4,2,1:T(8,128)} %get-tuple-element.323), channel_id=1, source_target_pairs={{16,0},{32,16},{48,32},{64,48},{80,64},{96,80},{112,96},{128,112},... | collective-permute-start | bytes 25928 | tf_op jit(solution)/shard_map/ppermute | solution.py:21
  49.3 2.3 copy-start.1
  54.1 10.7 %copy-start.15 = (s32[9]{0:T(128)S(1)}, s32[9]{0:T(128)}, u32[]{:S(2)}) copy-start(s32[9]{0:T(128)} %param.14) | copy-start | bytes 112
  54.1 14.4 %copy-start.6 = (f32[9,4,2,8,128]{4,0,3,2,1:T(8,128)S(1)}, f32[9,4,2,8,128]{4,0,3,2,1:T(8,128)}, u32[]{:S(2)}) copy-start(f32[9,4,2,8,128]{4,0,3,2,1:T(8,128)} %copy-done.5) | copy-start | bytes 884740
  57.6 56.4 %collective-permute-start.2 = (f32[9,5,2,3,128]{4,2,3,1,0:T(2,128)}, f32[9,5,2,3,128]{4,2,3,1,0:T(2,128)}, u32[]{:S(2)}, u32[]{:S(2)}) collective-permute-start(f32[9,5,2,3,128]{4,2,3,1,0:T(2,128)} %copy.150), channel_id=1, source_target_pairs={{2,0},{4,2},{6,4},{8,6},{10,8},{12,10},{14,12},{3,1},{5,3},{7,5},{... | collective-permute-start | bytes 414728 | tf_op jit(solution)/shard_map/ppermute | solution.py:21
  61.8 54.9 %collective-permute-start.3 = (f32[9,5,2,3,128]{4,2,3,1,0:T(2,128)}, f32[9,5,2,3,128]{4,2,3,1,0:T(2,128)}, u32[]{:S(2)}, u32[]{:S(2)}) collective-permute-start(f32[9,5,2,3,128]{4,2,3,1,0:T(2,128)} %copy.152), channel_id=1, source_target_pairs={{0,2},{2,4},{4,6},{6,8},{8,10},{10,12},{12,14},{1,3},{3,5},{5,7},{... | collective-permute-start | bytes 414728 | tf_op jit(solution)/shard_map/ppermute | solution.py:20
  70.1 10.1 %slice-start = ((s8[5242880]{0:T(1024)(128)(4,1)}), s8[4194304]{0:T(1024)(128)(4,1)S(1)}, s32[]{:S(2)}) async-start(s8[5242880]{0:T(1024)(128)(4,1)} %bitcast.138), calls=%async_computation.1 | async-start | bytes 8388608
  71.4 8.8 %slice-start.1 = ((s8[5242880]{0:T(1024)(128)(4,1)}), s8[1048576]{0:T(1024)(128)(4,1)S(1)}, s32[]{:S(2)}) async-start(s8[5242880]{0:T(1024)(128)(4,1)} %bitcast.138), calls=%async_computation.2 | async-start | bytes 2097152
  89.5 20.3 %copy-start.17 = (u32[256]{0:T(256)S(1)}, u32[256]{0:T(256)}, u32[]{:S(2)}) copy-start(u32[256]{0:T(256)} %constant.161) | copy-start | bytes 3076
  134.6 5.7 %copy-start.2 = (f32[9,5,8,2048]{3,0,2,1:T(8,128)S(1)}, f32[9,5,8,2048]{3,0,2,1:T(8,128)}, u32[]{:S(2)}) copy-start(f32[9,5,8,2048]{3,0,2,1:T(8,128)} %all-gather.4.cloned.1.call-done) | copy-start | bytes 8847364
  143.3 34.0 %copy-start.11 = (f32[9,5,2,8,1]{0,3,4,2,1:T(8,128)S(1)}, f32[9,5,2,8,1]{0,3,4,2,1:T(8,128)}, u32[]{:S(2)}) copy-start(f32[9,5,2,8,1]{0,3,4,2,1:T(8,128)} %get-tuple-element.330) | copy-start | bytes 8644
  213.2 3.4 copy-start.12
  213.2 88.5 %copy-start.13 = (f32[128,128]{1,0:T(8,128)S(1)}, f32[128,128]{1,0:T(8,128)}, u32[]{:S(2)}) copy-start(f32[128,128]{1,0:T(8,128)} %constant.152.clone) | copy-start | bytes 196612
  213.2 88.5 %copy-start.16 = (f32[128]{0:T(128)S(1)}, f32[128]{0:T(128)}, u32[]{:S(2)}) copy-start(f32[128]{0:T(128)} %constant.153.clone) | copy-start | bytes 1540
  213.2 170.4 %copy-start.14 = (f32[128]{0:T(128)S(1)}, f32[128]{0:T(128)}, u32[]{:S(2)}) copy-start(f32[128]{0:T(128)} %constant.154.clone) | copy-start | bytes 1540
  216.6 167.9 %copy-start.7 = (f32[9,5,2,8,128]{4,3,2,1,0:T(8,128)}, f32[9,5,2,8,128]{4,3,2,1,0:T(8,128)S(1)}, u32[]{:S(2)}) copy-start(f32[9,5,2,8,128]{4,3,2,1,0:T(8,128)S(1)} %copy.159) | copy-start | bytes 1105924
Sparse Core Ops, SparseCore 0:
  34.8 99.7 all-gather.3
where the time goes:
time: 393 us; the launch traced here: 391 us
  local copies, waits for them, and re-layouts  128 us (33%)
  blocking collectives  123 us (31%)
  other arithmetic  77 us (20%)
  between operations  31.6 us (8%)
  waiting for transfers between devices  14.6 us (4%)
  starting transfers between devices  13.3 us (3%)
    unnamed x2, blocking collectives  123 us
    add x1, other arithmetic, local(): residual + penalty[:, :, None] * chosen[None, None, :, None, None]  35.9 us
    unnamed x58, local copies, waits for them, and re-layouts  23.9 us
    slice x5, local copies, waits for them, and re-layouts, pitch_derivative(): jnp.roll(along_pitch, reach, axis=4)  21.1 us
    slice x1, local copies, waits for them, and re-layouts, cut_rows(): joined[member]  20.9 us
    select_n x32, other arithmetic, hop(): return jax.tree.map(lambda a, b: jnp.where(reached, a, b), new, before)  20.8 us
    dynamic_slice x64, local copies, waits for them, and re-layouts, hop(): new = combine(before, jax.tree.map(lambda part: part[at], everything))  19.5 us
    all_gather x1, waiting for transfers between devices, local(): whole = lax.all_gather(facing, 'pitch', axis=3, tiled=True)  14.6 us
  transfers between devices with their start and end apart: 6, of which 1 were waited for; matrix products, arithmetic and copies ran while one was open for 20% of the time, Pallas kernels for 0%

commit v1 on v0

--- a/solution.py
+++ b/solution.py
@@ -189,7 +189,9 @@
     facing = from_partner(edge, "axial", 0)
     extent = width * count_p
     offsets = jnp.where(stator, shifts, (extent - shifts) % extent)
-    whole = lax.all_gather(facing, "pitch", axis=3, tiled=True)
+    whole = jnp.concatenate(
+        lax.all_to_all(jnp.stack([facing] * lax.axis_size("pitch")), "pitch", 0, 0), axis=3
+    )
     joined = jnp.concatenate([whole, whole], axis=3)
     aligned = cut_rows(joined, (place * width - offsets) % extent, width)
     penalty = aligned - edge

time: 393 us -> 347 us (0.88)
  local copies, waits for them, and re-layouts: 128 us -> 103 us
  waiting for transfers between devices: 14.6 us -> 0.02 us
  between operations: 31.6 us -> 18.4 us
  starting transfers between devices: 13.3 us -> 20.4 us
    slice x1, local copies, waits for them, and re-layouts: 20.9 us -> 0.67 us  [cut_rows(): joined[member]]
    all_gather x1 -> x0, waiting for transfers between devices: 14.6 us -> none  [local(): whole = lax.all_gather(facing, 'pitch', axis=3, tiled=True)]
    all_to_all x0 -> x1, starting transfers between devices: none -> 8.64 us  [local(): lax.all_to_all(jnp.stack([facing] * lax.axis_size('pitch')), 'pitch', 0, 0)]
    another operation x6 -> x1, local copies, waits for them, and re-layouts: 9.02 us -> 1.82 us  [cut_rows(): return jnp.stack(pieces, axis=0)]
    unnamed x58 -> x52, local copies, waits for them, and re-layouts: 23.9 us -> 17.4 us
    slice x2, local copies, waits for them, and re-layouts: 6.06 us -> 10 us  [padded_2(): leading = lax.slice_in_dim(x, 0, width, axis=dim)]
  transfers between devices with their start and end apart: 6 -> 6, of which waited for: 1 -> 0; matrix products, arithmetic and copies ran while one was open for 20% -> 24% of each run, Pallas kernels for 0% -> 0%
where the time goes in v1:
time: 347 us; the launch traced here: 344 us
  blocking collectives  122 us (35%)
  local copies, waits for them, and re-layouts  103 us (30%)
  other arithmetic  77.7 us (22%)
  starting transfers between devices  20.4 us (6%)
  between operations  18.4 us (5%)
    unnamed x2, blocking collectives  122 us
    add x1, other arithmetic, local(): residual + penalty[:, :, None] * chosen[None, None, :, None, None]  35.9 us
    slice x5, local copies, waits for them, and re-layouts, pitch_derivative(): jnp.roll(along_pitch, reach, axis=4)  20.9 us
    select_n x32, other arithmetic, hop(): return jax.tree.map(lambda a, b: jnp.where(reached, a, b), new, before)  20.8 us
    dynamic_slice x64, local copies, waits for them, and re-layouts, hop(): new = combine(before, jax.tree.map(lambda part: part[at], everything))  19.5 us
    unnamed x52, local copies, waits for them, and re-layouts  17.4 us
    slice x2, local copies, waits for them, and re-layouts, padded_2(): leading = lax.slice_in_dim(x, 0, width, axis=dim)  10 us
    unnamed x7, other arithmetic  9.26 us
  transfers between devices with their start and end apart: 6, of which 0 were waited for; matrix products, arithmetic and copies ran while one was open for 24% of the time, Pallas kernels for 0%

profile of v1, /device:TPU:8, one launch (start us, length us, event | category | flops | bytes accessed | tf_op | source)
XLA Modules:
  0.0 344.4 jit_solution(3395495685797877515)
XLA Ops:
  0.6 1.1 copy.183
  1.8 1.0 copy.199
  2.8 3.1 collective-permute-start.4
  6.0 1.7 fusion.59
  7.6 1.3 copy.171
  9.3 1.0 constant_dynamic-update-slice_fusion
  10.4 1.4 copy.192
  11.7 1.3 copy.193
  13.0 1.0 constant_dynamic-update-slice_fusion.1
  14.1 2.3 fusion.24
  16.4 2.2 copy.174
  18.6 2.4 bitcast_dynamic-update-slice_fusion.9
  21.0 2.8 bitcast_dynamic-update-slice_fusion.8
  23.8 0.7 multiply_divide_fusion
  24.4 2.3 copy.176
  26.7 1.3 copy.194
  28.0 1.0 copy.185
  29.0 1.8 stack.89
  30.8 8.6 %all-to-all-start = ((f32[16,9,5,8,128]{4,3,2,1,0:T(8,128)}), f32[16,9,5,8,128]{4,3,2,1,0:T(8,128)}, u32[]{:S(2)}, u32[]{:S(2)}) async-start(f32[16,9,5,8,128]{4,3,2,1,0:T(8,128)} %stack.89), calls=%async_computation | async-start | bytes 5898240 | tf_op jit(solution)/shard_map/all_to_all | solution.py:193
  39.5 2.9 bitcast_dynamic-update-slice_fusion.7
  42.4 1.8 bitcast_dynamic-update-slice_fusion.6
  44.2 1.7 fusion.52
  45.8 1.9 collective-permute-start
  47.7 2.3 collective-permute-start.1
  50.0 1.2 bitcast_dynamic-update-slice_fusion.3
  51.2 1.3 bitcast_dynamic-update-slice_fusion.2
  52.5 6.5 %fusion.58 = (f32[9,5,2,3,128]{0,3,4,2,1:T(4,128)}, f32[9,5,2,3,128]{0,3,4,2,1:T(4,128)S(1)}) fusion(f32[9,5,2,8,128]{0,3,4,2,1:T(8,128)} %bitcast_dynamic-update-slice_fusion.2), kind=kLoop, calls=%fused_computation.143 | loop fusion | bytes 552960 | tf_op jit(solution)/shard_map/slice | solution.py:19
  59.0 3.5 %copy.178 = f32[9,5,2,3,128]{4,2,3,1,0:T(2,128)} copy(f32[9,5,2,3,128]{0,3,4,2,1:T(4,128)} %get-tuple-element.336) | data formatting | bytes 276480 | tf_op jit(solution)/shard_map/slice | solution.py:19
  62.5 1.9 collective-permute-start.2
  64.4 2.2 copy.180
  66.7 2.6 collective-permute-start.3
  69.9 0.7 fusion.60
  70.6 1.4 fusion.56
  72.0 1.6 fusion.54
  73.6 1.6 fusion.27
  75.2 1.3 fusion.51
  76.5 8.7 %fusion.53 = (f32[9,5,2,8,125]{0,3,4,2,1:T(8,128)}, f32[9,5,2,8,125]{0,3,4,2,1:T(8,128)}) fusion(f32[9,5,2,8,128]{0,3,4,2,1:T(8,128)} %get-tuple-element.338), kind=kLoop, calls=%fused_computation.138 | loop fusion | bytes 1440000 | tf_op jit(solution)/shard_map/jit(_roll_static)/slice | solution.py:106
  85.2 4.6 %fusion.55 = (f32[9,5,2,8,126]{0,3,4,2,1:T(8,128)}, f32[9,5,2,8,126]{0,3,4,2,1:T(8,128)}) fusion(f32[9,5,2,8,128]{0,3,4,2,1:T(8,128)S(1)} %bitcast.139), kind=kLoop, calls=%fused_computation.140 | loop fusion | bytes 1451520 | tf_op jit(solution)/shard_map/jit(_roll_static)/slice | solution.py:106
  89.7 4.6 %fusion.57 = (f32[9,5,2,8,127]{0,3,4,2,1:T(8,128)}, f32[9,5,2,8,127]{0,3,4,2,1:T(8,128)}) fusion(f32[9,5,2,8,128]{0,3,4,2,1:T(8,128)S(1)} %bitcast.139), kind=kLoop, calls=%fused_computation.142 | loop fusion | bytes 1463040 | tf_op jit(solution)/shard_map/jit(_roll_static)/slice | solution.py:106
  106.1 3.1 copy.184
  116.1 0.7 dynamic-update-slice.1
  116.8 2.1 fusion.42
  118.9 2.7 copy.179
  121.6 3.4 copy.181
  124.9 2.2 bitcast_dynamic-update-slice_fusion
  127.1 2.2 bitcast_dynamic-update-slice_fusion.1
  129.4 0.7 fusion.50
  130.1 0.7 constant_dynamic-slice_fusion.8
  130.8 0.7 constant_dynamic-slice_fusion.6
  131.5 0.7 constant_dynamic-slice_fusion.4
  132.2 0.7 constant_dynamic-slice_fusion.2
  132.9 1.8 stack.99
  134.7 0.8 subtract_bitcast_fusion
  135.5 3.2 copy.187
  138.7 35.9 %fusion.7 = f32[9,5,2,8,128]{0,3,4,2,1:T(8,128)} fusion(f32[9,5,2,8,128]{0,3,4,2,1:T(8,128)} %copy.184, f32[9,5,2,8,128]{0,3,4,2,1:T(8,128)} %bitcast_dynamic-update-slice_fusion.2, f32[9,5,2,3,128]{0,3,4,2,1:T(4,128)} %copy.181, f32[9,5,2,3,128]{0,3,4,2,1:T(4,128)S(1)} %copy.179, f32[9,5,2,8,1]{0,3,4,2,1:T(8,128)} %get-tuple-element.333, ...), kind=kLoop, calls=%fused_computation.21 | loop fusion | flops 3133440 | bytes 3796104 | tf_op jit(solution)/shard_map/add | solution.py:200
  174.7 3.4 copy.189
  179.2 61.7 %all-reduce.6 = (f32[11520]{0:T(1024)S(1)}, f32[16]{0:T(128)S(1)}, f32[720]{0:T(1024)S(1)}) all-reduce(f32[11520]{0:T(1024)S(1)} %dynamic-update-slice, f32[16]{0:T(128)S(1)} %dynamic-update-slice.1, f32[720]{0:T(1024)S(1)} %get-tuple-element.284), channel_id=2, replica_groups=mesh['pitch'=16,'radial'=8,'axial'=2] {'pitch'}, use_global_device_ids=true, to_apply=%add.2 | all-reduce | flops 12256 | bytes 98048
  241.0 20.6 %while.30 = (s32[]{:T(128)}, f32[720]{0:T(1024)S(1)}, s32[]{:T(128)}, f32[16,720]{1,0:T(8,128)S(1)}, f32[16,1]{0,1:T(1,128)S(1)}, /*index=5*/s32[]{:T(128)}, s32[]{:T(128)}) while((s32[]{:T(128)}, f32[720]{0:T(1024)S(1)}, s32[]{:T(128)}, f32[16,720]{1,0:T(8,128)S(1)}, f32[16,1]{0,1:T(1,128)S(1)}, /*index=5*/s32[]{:T(128)}, ...), condition=%wide.region_1.2_spmd.clone, body=%wide.region_0.1_spmd.clone.sunk | while | flops 2884 | bytes 14517 | solution.py:39
  241.6 0.7 add_select_fusion.4
  242.9 0.7 add_select_fusion.4
  253.2 0.7 add_select_fusion.4
  262.7 59.9 %all-reduce.5 = (f32[11520]{0:T(1024)S(1)}, f32[720]{0:T(1024)S(1)}) all-reduce(f32[11520]{0:T(1024)S(1)} %dynamic-update-slice.2, f32[720]{0:T(1024)S(1)} %get-tuple-element.282), channel_id=3, replica_groups=mesh['pitch'=16,'radial'=8,'axial'=2] {'pitch'}, use_global_device_ids=true, to_apply=%add.4 | all-reduce | flops 12240 | bytes 97920
  322.8 20.7 %while.31 = (s32[]{:T(128)}, f32[720]{0:T(1024)S(1)}, s32[]{:T(128)}, f32[16,720]{1,0:T(8,128)S(1)}, f32[16,1]{0,1:T(1,128)S(1)}, /*index=5*/s32[]{:T(128)}, s32[]{:T(128)}, s32[]{:T(128)}, s32[]{:T(128)}) while((s32[]{:T(128)}, f32[720]{0:T(1024)S(1)}, s32[]{:T(128)}, f32[16,720]{1,0:T(8,128)S(1)}, f32[16,1]{0,1:T(1,128)S(1)}, ...), condition=%wide.region_4.5_spmd.clone, body=%wide.region_3.4_spmd.clone.sunk | while | flops 2888 | bytes 14579 | solution.py:39
  343.5 0.9 add_multiply_fusion
  (156 shorter events, 43.2 us)
Async XLA Ops:
  1.8 4.2 %copy-start.2 = (f32[9,4,2,8,128]{4,0,3,2,1:T(8,128)}, f32[9,4,2,8,128]{4,0,3,2,1:T(8,128)S(1)}, u32[]{:S(2)}) copy-start(f32[9,4,2,8,128]{4,0,3,2,1:T(8,128)S(1)} %copy.183) | copy-start | bytes 884740
  2.8 3.2 copy-start.5
  2.8 25.2 %collective-permute-start.4 = (f32[9,5,8,128]{3,0,2,1:T(8,128)S(1)}, f32[9,5,8,128]{3,0,2,1:T(8,128)}, u32[]{:S(2)}, u32[]{:S(2)}) collective-permute-start(f32[9,5,8,128]{3,0,2,1:T(8,128)S(1)} %bitcast.141), channel_id=1, source_target_pairs={{0,1},{1,0},{2,3},{3,2},{4,5},{5,4},{6,7},{7,6},{8,9},{9,8},{10,11... | collective-permute-start | bytes 552968 | tf_op jit(solution)/shard_map/ppermute | solution.py:43
  18.6 5.2 %copy-start.6 = (f32[9,2,8,128]{3,2,1,0:T(8,128)S(1)}, f32[9,2,8,128]{3,2,1,0:T(8,128)}, u32[]{:S(2)}) copy-start(f32[9,2,8,128]{3,2,1,0:T(8,128)} %param.12) | copy-start | bytes 221188
  18.6 5.2 %copy-start.7 = (f32[9,2,8,128]{3,2,1,0:T(8,128)S(1)}, f32[9,2,8,128]{3,2,1,0:T(8,128)}, u32[]{:S(2)}) copy-start(f32[9,2,8,128]{3,2,1,0:T(8,128)} %copy.174) | copy-start | bytes 221188
  30.8 94.1 %all-to-all-start = ((f32[16,9,5,8,128]{4,3,2,1,0:T(8,128)}), f32[16,9,5,8,128]{4,3,2,1,0:T(8,128)}, u32[]{:S(2)}, u32[]{:S(2)}) async-start(f32[16,9,5,8,128]{4,3,2,1,0:T(8,128)} %stack.89), calls=%async_computation | async-start | bytes 5898240 | tf_op jit(solution)/shard_map/all_to_all | solution.py:193
  39.5 2.9 copy-start
  39.5 2.9 copy-start.1
  45.8 70.9 %collective-permute-start = (f32[9,5,2,8,3]{0,3,4,2,1:T(8,128)}, f32[9,5,2,8,3]{0,3,4,2,1:T(8,128)}, u32[]{:S(2)}, u32[]{:S(2)}) collective-permute-start(f32[9,5,2,8,3]{0,3,4,2,1:T(8,128)} %get-tuple-element.324), channel_id=1, source_target_pairs={{0,16},{16,32},{32,48},{48,64},{64,80},{80,96},{96,112},{112,128},... | collective-permute-start | bytes 25928 | tf_op jit(solution)/shard_map/ppermute | solution.py:20
  47.7 69.1 %collective-permute-start.1 = (f32[9,5,2,8,3]{0,3,4,2,1:T(8,128)}, f32[9,5,2,8,3]{0,3,4,2,1:T(8,128)}, u32[]{:S(2)}, u32[]{:S(2)}) collective-permute-start(f32[9,5,2,8,3]{0,3,4,2,1:T(8,128)} %get-tuple-element.325), channel_id=1, source_target_pairs={{16,0},{32,16},{48,32},{64,48},{80,64},{96,80},{112,96},{128,112},... | collective-permute-start | bytes 25928 | tf_op jit(solution)/shard_map/ppermute | solution.py:21
  59.0 10.8 %copy-start.12 = (s32[9]{0:T(128)S(1)}, s32[9]{0:T(128)}, u32[]{:S(2)}) copy-start(s32[9]{0:T(128)} %param.14) | copy-start | bytes 112
  59.0 14.6 %copy-start.3 = (f32[9,4,2,8,128]{4,0,3,2,1:T(8,128)S(1)}, f32[9,4,2,8,128]{4,0,3,2,1:T(8,128)}, u32[]{:S(2)}) copy-start(f32[9,4,2,8,128]{4,0,3,2,1:T(8,128)} %copy-done.2) | copy-start | bytes 884740
  62.5 56.4 %collective-permute-start.2 = (f32[9,5,2,3,128]{4,2,3,1,0:T(2,128)}, f32[9,5,2,3,128]{4,2,3,1,0:T(2,128)}, u32[]{:S(2)}, u32[]{:S(2)}) collective-permute-start(f32[9,5,2,3,128]{4,2,3,1,0:T(2,128)} %copy.178), channel_id=1, source_target_pairs={{2,0},{4,2},{6,4},{8,6},{10,8},{12,10},{14,12},{3,1},{5,3},{7,5},{... | collective-permute-start | bytes 414728 | tf_op jit(solution)/shard_map/ppermute | solution.py:21
  66.7 54.9 %collective-permute-start.3 = (f32[9,5,2,3,128]{4,2,3,1,0:T(2,128)}, f32[9,5,2,3,128]{4,2,3,1,0:T(2,128)}, u32[]{:S(2)}, u32[]{:S(2)}) collective-permute-start(f32[9,5,2,3,128]{4,2,3,1,0:T(2,128)} %copy.180), channel_id=1, source_target_pairs={{0,2},{2,4},{4,6},{6,8},{8,10},{10,12},{12,14},{1,3},{3,5},{5,7},{... | collective-permute-start | bytes 414728 | tf_op jit(solution)/shard_map/ppermute | solution.py:20
  75.2 10.0 %slice-start = ((s8[5242880]{0:T(1024)(128)(4,1)}), s8[4194304]{0:T(1024)(128)(4,1)S(1)}, s32[]{:S(2)}) async-start(s8[5242880]{0:T(1024)(128)(4,1)} %bitcast.138), calls=%async_computation.1 | async-start | bytes 8388608
  76.4 8.7 %slice-start.1 = ((s8[5242880]{0:T(1024)(128)(4,1)}), s8[1048576]{0:T(1024)(128)(4,1)S(1)}, s32[]{:S(2)}) async-start(s8[5242880]{0:T(1024)(128)(4,1)} %bitcast.138), calls=%async_computation.2 | async-start | bytes 2097152
  94.4 20.6 %copy-start.14 = (u32[256]{0:T(256)S(1)}, u32[256]{0:T(256)}, u32[]{:S(2)}) copy-start(u32[256]{0:T(256)} %constant.161) | copy-start | bytes 3076
  129.3 9.4 %copy-start.8 = (f32[9,5,2,8,1]{0,3,4,2,1:T(8,128)S(1)}, f32[9,5,2,8,1]{0,3,4,2,1:T(8,128)}, u32[]{:S(2)}) copy-start(f32[9,5,2,8,1]{0,3,4,2,1:T(8,128)} %get-tuple-element.332) | copy-start | bytes 8644
  174.6 3.4 copy-start.9
  174.6 87.0 %copy-start.10 = (f32[128,128]{1,0:T(8,128)S(1)}, f32[128,128]{1,0:T(8,128)}, u32[]{:S(2)}) copy-start(f32[128,128]{1,0:T(8,128)} %constant.152.clone) | copy-start | bytes 196612
  174.6 87.0 %copy-start.13 = (f32[128]{0:T(128)S(1)}, f32[128]{0:T(128)}, u32[]{:S(2)}) copy-start(f32[128]{0:T(128)} %constant.153.clone) | copy-start | bytes 1540
  174.6 168.9 %copy-start.11 = (f32[128]{0:T(128)S(1)}, f32[128]{0:T(128)}, u32[]{:S(2)}) copy-start(f32[128]{0:T(128)} %constant.154.clone) | copy-start | bytes 1540
  178.0 166.4 %copy-start.4 = (f32[9,5,2,8,128]{4,3,2,1,0:T(8,128)}, f32[9,5,2,8,128]{4,3,2,1,0:T(8,128)S(1)}, u32[]{:S(2)}) copy-start(f32[9,5,2,8,128]{4,3,2,1,0:T(8,128)S(1)} %copy.189) | copy-start | bytes 1105924
